TPU v7x, 32 devices: a whole 2x2x4 slice. The times are simulated.
32 devices in a mesh: row: 8 (over z, x), col: 4 (over y, core).
Axes of the slice: x: 2, y: 2, z: 4, core: 2. Of those that a mesh axis runs over, the one named last changes fastest.
Arguments:
- start_vec: float32 [4, 1024, 256], P(None, 'row'), may hold values from -6.2 to 6.2
- cond_orb: bfloat16 [1024, 16384], P('row', 'col'), may hold values from -6 to 6
- val_orb: bfloat16 [256, 16384], P('row', 'col'), may hold values from -6 to 6
- kernel: float32 [16384, 16384], P('row', 'col'), may hold values from -7.1525574e-07 to 7.1525574e-07
- cond_energy: float32 [1024], P('row'), may hold values from 1 to 3
- val_energy: float32 [256], replicated, may hold values from -2 to 0
Outputs:
- right_next: float32 [4, 1024, 256], P(None, 'row')
- left_next: float32 [4, 1024, 256], P(None, 'row')
- coefs: float32 [4, 4], replicated
All inputs are finite; a program needn't handle non-finite values.
Results may differ from a plain program's by a relative error of at most 0.0046.
Values may be sent and summed in bfloat16 or wider, within the bound.
A program may use at most 128 MiB of HBM per device.

v0:
```python
import jax
import jax.numpy as jnp
from jax import lax
from jax.sharding import PartitionSpec as P

ITERS = 2


def inner_local(first, second):
    return jnp.sum(first * second, axis=(1, 2))


def shards(start_vec, cond_orb, val_orb, kernel, cond_energy, val_energy):
    count = start_vec.shape[0]
    row_place = lax.axis_index("row")
    col_place = lax.axis_index("col")
    span_row = kernel.shape[0]
    span_col = kernel.shape[1]
    panel = lax.all_gather(val_orb, "row", axis=0, tiled=True)
    cond_f = cond_orb.astype(jnp.float32)
    energy = cond_energy[:, None] - val_energy[None, :]

    def row_total(values):
        return lax.psum(values, "row")

    def col_total(values):
        return lax.psum(values, "col")

    def reduce_dots(terms):
        return row_total(terms)

    (norm_sq,) = reduce_dots((inner_local(start_vec, start_vec),))
    right = start_vec / jnp.sqrt(norm_sq)[:, None, None]
    left = right
    right_old = jnp.zeros_like(right)
    left_old = jnp.zeros_like(left)
    record = []
    for step in range(ITERS):
        stack = jnp.concatenate([right, left], axis=0)
        rounded = stack.astype(jnp.bfloat16)
        paired = jnp.einsum("bcv,vn->bcn", rounded, panel, preferred_element_type=jnp.float32)
        partial_value = jnp.sum(paired * cond_f[None], axis=1)
        folded = row_total(partial_value)
        right_coeff = folded[:count]
        left_coeff = folded[count:]
        left_all = lax.all_gather(left_coeff, "col", axis=1, tiled=True)
        left_rows = lax.dynamic_slice_in_dim(left_all, row_place * span_row, span_row, 1)
        right_part = jnp.einsum(
            "bn,mn->bm",
            right_coeff,
            kernel,
            precision=lax.Precision.HIGHEST,
            preferred_element_type=jnp.float32,
        )
        left_part = jnp.einsum(
            "bm,mn->bn",
            left_rows,
            kernel,
            precision=lax.Precision.HIGHEST,
            preferred_element_type=jnp.float32,
        )
        right_zed = col_total(right_part)
        left_zed = row_total(left_part)
        right_all = lax.all_gather(right_zed, "row", axis=1, tiled=True)
        right_cols = lax.dynamic_slice_in_dim(right_all, col_place * span_col, span_col, 1)
        zed = jnp.concatenate([right_cols, left_zed], axis=0)
        weighted = (cond_f[None] * zed[:, None, :]).astype(jnp.bfloat16)
        image_terms = jnp.einsum("bcn,vn->bcv", weighted, panel, preferred_element_type=jnp.float32)
        kernel_part = col_total(image_terms)
        images = energy[None] * stack + kernel_part
        image_r = images[:count]
        image_l = images[count:]
        table = reduce_dots(
            (
                inner_local(left, image_r),
                inner_local(left_old, image_r),
                inner_local(right_old, image_l),
                inner_local(image_l, image_r),
                inner_local(image_l, right),
                inner_local(left, right),
                inner_local(left, right_old),
                inner_local(left_old, right),
                inner_local(left_old, right_old),
                inner_local(image_r, image_r),
                inner_local(right, right),
                inner_local(right_old, right_old),
                inner_local(image_r, right),
                inner_local(image_r, right_old),
                inner_local(right, right_old),
                inner_local(image_l, image_l),
                inner_local(left, left),
                inner_local(left_old, left_old),
                inner_local(image_l, left),
                inner_local(image_l, left_old),
                inner_local(left, left_old),
            )
        )
        alpha, mu_co, nu_co = (table[0], table[1], table[2])
        cross = (
            table[3]
            - alpha * table[4]
            - mu_co * nu_co
            - alpha * alpha
            + alpha * alpha * table[5]
            + alpha * mu_co * table[6]
            - nu_co * mu_co
            + nu_co * alpha * table[7]
            + nu_co * mu_co * table[8]
        )
        right_sq = (
            table[9]
            + alpha * alpha * table[10]
            + mu_co * mu_co * table[11]
            - 2.0 * alpha * table[12]
            - 2.0 * mu_co * table[13]
            + 2.0 * alpha * mu_co * table[14]
        )
        left_sq = (
            table[15]
            + alpha * alpha * table[16]
            + nu_co * nu_co * table[17]
            - 2.0 * alpha * table[18]
            - 2.0 * nu_co * table[19]
            + 2.0 * alpha * nu_co * table[20]
        )
        resid_r = image_r - alpha[:, None, None] * right - mu_co[:, None, None] * right_old
        resid_l = image_l - alpha[:, None, None] * left - nu_co[:, None, None] * left_old
        bound = jnp.maximum(cross, 0.25 * jnp.sqrt(right_sq * left_sq))
        beta = jnp.sqrt(bound)
        right_old, left_old = (right, left)
        right = resid_r / beta[:, None, None]
        left = resid_l / beta[:, None, None]
        record.append(alpha)
        record.append(beta)
    joined = jnp.concatenate([right, left], axis=0)
    return (joined[:count], joined[count:], jnp.stack(record, axis=1))


def solution(mesh):
    in_specs = (
        P(None, "row", None),
        P("row", "col"),
        P("row", "col"),
        P("row", "col"),
        P("row"),
        P(),
    )
    out_specs = (P(None, "row", None), P(None, "row", None), P())
    return jax.shard_map(shards, mesh=mesh, in_specs=in_specs, out_specs=out_specs, check_vma=False)
```

profile of v0, /device:TPU:0, one launch (start us, length us, event | category | flops | bytes accessed | tf_op | source)
XLA Modules:
  0.0 696.7 jit_solution(7702828780457576964)
XLA Ops:
  7.9 1.2 multiply_reduce_fusion.25
  9.1 23.4 %psum.214 = f32[4]{0:T(128)S(1)} all-reduce(f32[4]{0:T(128)S(1)} %multiply_reduce_fusion.25), channel_id=1, replica_groups=mesh['row'=8,'col'=4] {'row'}, use_global_device_ids=true, to_apply=%region_1.0 | all-reduce | flops 4 | bytes 32 | tf_op jit(solution)/shard_map/psum | solution.py:24
  32.6 1.4 convert_element_type.15
  34.0 1.5 broadcast_divide_fusion
  35.6 26.6 %all-gather.2.cloned.1.call-done = bf16[256,4096]{1,0:T(8,128)(2,1)} async-done(((bf16[32,4096]{1,0:T(8,128)(2,1)}), bf16[256,4096]{1,0:T(8,128)(2,1)}) %all-gather.2.cloned.1.call-update) | async-done | bytes 2097168 | tf_op jit(solution)/shard_map/all_gather | solution.py:19
  62.2 4.6 multiply_reduce_fusion.1
  67.0 68.9 %all-reduce.9.cloned.1.call-done = f32[8,4096]{1,0:T(8,128)} async-done(((f32[8,4096]{1,0:T(8,128)}), f32[8,4096]{1,0:T(8,128)}) %all-reduce.9.cloned.1.call-update) | async-done | bytes 131088 | tf_op jit(solution)/shard_map/psum | solution.py:24
  136.0 37.3 %fusion.18 = f32[4,2048]{1,0:T(4,128)S(1)} fusion(f32[2048,4096]{1,0:T(8,128)} %param.9, f32[8,4096]{1,0:T(8,128)} %all-reduce.9.cloned.1.call-done), kind=kOutput, calls=%fused_computation.54 | convolution fusion | flops 402653184 | bytes 33652736 | tf_op jit(solution)/shard_map/bn,mn->bm/dot_general | solution.py:48
  173.3 10.3 %psum.216 = f32[4,2048]{1,0:T(4,128)S(1)} all-reduce(f32[4,2048]{1,0:T(4,128)S(1)} %fusion.18), channel_id=1, replica_groups=mesh['row'=8,'col'=4] {'col'}, use_global_device_ids=true, to_apply=%region_4.0 | all-reduce | flops 8192 | bytes 65536 | tf_op jit(solution)/shard_map/psum | solution.py:27
  183.6 30.8 %all_gather.16 = f32[4,16384]{1,0:T(4,128)S(1)} all-gather(f32[4,2048]{1,0:T(4,128)S(1)} %psum.216), channel_id=1, replica_groups=mesh['row'=8,'col'=4] {'row'}, dimensions={1}, use_global_device_ids=true | all-gather | bytes 294912 | tf_op jit(solution)/shard_map/all_gather | solution.py:64
  214.4 6.2 all_gather.17
  220.6 20.1 %fusion.22 = f32[4,4096]{1,0:T(4,128)} fusion(f32[2048,4096]{1,0:T(8,128)} %param.9, f32[4,16384]{1,0:T(4,128)S(1)} %all_gather.17, s32[]{:T(128)S(6)} %select_n.9), kind=kOutput, calls=%fused_computation.59 | convolution fusion | flops 402653184 | bytes 33652740 | tf_op jit(solution)/shard_map/bm,mn->bn/dot_general | solution.py:55
  240.8 68.4 %all-reduce.11.cloned.1.call-done = f32[4,4096]{1,0:T(4,128)} async-done(((f32[4,4096]{1,0:T(4,128)}), f32[4,4096]{1,0:T(4,128)}) %all-reduce.11.cloned.1.call-update) | async-done | bytes 65552 | tf_op jit(solution)/shard_map/psum | solution.py:24
  309.2 0.9 pad_maximum_fusion.2
  310.1 5.0 fusion
  315.2 36.2 %all-reduce.13.cloned.1.call-done = f32[8,128,256]{2,1,0:T(8,128)} async-done(((f32[8,128,256]{2,1,0:T(8,128)}), f32[8,128,256]{2,1,0:T(8,128)}) %all-reduce.13.cloned.1.call-update) | async-done | bytes 1048592 | tf_op jit(solution)/shard_map/psum | solution.py:27
  351.5 1.4 fusion.12
  353.3 21.6 %all-reduce.1 = (f32[4]{0:T(128)S(1)}, f32[4]{0:T(128)S(1)}, f32[4]{0:T(128)S(1)}, f32[4]{0:T(128)S(1)}, f32[4]{0:T(128)S(1)}, /*index=5*/f32[4]{0:T(128)S(1)}, f32[4]{0:T(128)S(1)}, f32[4]{0:T(128)S(1)}, f32[4]{0:T(128)S(1)}) all-reduce(f32[4]{0:T(128)S(1)} %get-tuple-element.33, ...), channel_id=1, replica_groups=mesh['row'=8,'col'=4] {'row'}, use_global_device_ids=true, to_apply=%region_20.0 | all-reduce | flops 36 | bytes 288 | tf_op jit(solution)/shard_map/psum | solution.py:24
  375.2 5.3 multiply_reduce_fusion
  380.9 67.1 %all-reduce.15.cloned.1.call-done = f32[8,4096]{1,0:T(8,128)} async-done(((f32[8,4096]{1,0:T(8,128)}), f32[8,4096]{1,0:T(8,128)}) %all-reduce.15.cloned.1.call-update) | async-done | bytes 131088 | tf_op jit(solution)/shard_map/psum | solution.py:24
  448.0 37.3 %fusion.16 = f32[4,2048]{1,0:T(4,128)S(1)} fusion(f32[2048,4096]{1,0:T(8,128)} %param.9, f32[8,4096]{1,0:T(8,128)} %all-reduce.15.cloned.1.call-done), kind=kOutput, calls=%fused_computation.52 | convolution fusion | flops 402653184 | bytes 33652736 | tf_op jit(solution)/shard_map/bn,mn->bm/dot_general | solution.py:48
  485.3 10.3 %psum.239 = f32[4,2048]{1,0:T(4,128)S(1)} all-reduce(f32[4,2048]{1,0:T(4,128)S(1)} %fusion.16), channel_id=1, replica_groups=mesh['row'=8,'col'=4] {'col'}, use_global_device_ids=true, to_apply=%region_27.0 | all-reduce | flops 8192 | bytes 65536 | tf_op jit(solution)/shard_map/psum | solution.py:27
  495.6 30.8 %all_gather.18 = f32[4,16384]{1,0:T(4,128)S(1)} all-gather(f32[4,2048]{1,0:T(4,128)S(1)} %psum.239), channel_id=1, replica_groups=mesh['row'=8,'col'=4] {'row'}, dimensions={1}, use_global_device_ids=true | all-gather | bytes 294912 | tf_op jit(solution)/shard_map/all_gather | solution.py:64
  526.4 6.2 all_gather.19
  532.5 20.1 %fusion.20 = f32[4,4096]{1,0:T(4,128)} fusion(f32[2048,4096]{1,0:T(8,128)} %param.9, f32[4,16384]{1,0:T(4,128)S(1)} %all_gather.19, s32[]{:T(128)S(6)} %select_n.9), kind=kOutput, calls=%fused_computation.57 | convolution fusion | flops 402653184 | bytes 33652740 | tf_op jit(solution)/shard_map/bm,mn->bn/dot_general | solution.py:55
  552.8 68.4 %all-reduce.17.cloned.1.call-done = f32[4,4096]{1,0:T(4,128)} async-done(((f32[4,4096]{1,0:T(4,128)}), f32[4,4096]{1,0:T(4,128)}) %all-reduce.17.cloned.1.call-update) | async-done | bytes 65552 | tf_op jit(solution)/shard_map/psum | solution.py:24
  621.2 0.9 pad_maximum_fusion.3
  622.0 5.6 fusion.1
  627.6 36.4 %all-reduce.19.cloned.1.call-done = f32[8,128,256]{2,1,0:T(8,128)} async-done(((f32[8,128,256]{2,1,0:T(8,128)}), f32[8,128,256]{2,1,0:T(8,128)}) %all-reduce.19.cloned.1.call-update) | async-done | bytes 1048592 | tf_op jit(solution)/shard_map/psum | solution.py:27
  664.0 1.4 multiply_add_fusion
  666.1 21.6 %all-reduce = (f32[4]{0:T(128)S(1)}, f32[4]{0:T(128)S(1)}, f32[4]{0:T(128)S(1)}, f32[4]{0:T(128)S(1)}, f32[4]{0:T(128)S(1)}, /*index=5*/f32[4]{0:T(128)S(1)}, f3...) all-reduce(f32[4]{0:T(128)S(1)} %get-tuple-element.18, ...), channel_id=1, replica_groups=mesh['row'=8,'col'=4] {'row'}, use_global_device_ids=true, to_apply=%region_45.0 | all-reduce | flops 56 | bytes 448 | tf_op jit(solution)/shard_map/psum | solution.py:24
  687.7 1.3 subtract_divide_fusion
  (39 shorter events, 4.0 us)
Async XLA Ops:
  7.2 55.0 %all-gather.2.cloned.1.call-start = ((), (), s32[]{:S(2)}) async-start(), calls=%async_computation | async-start | bytes 2359296 | tf_op jit(solution)/shard_map/all_gather | solution.py:19
  7.9 128.1 %all-reduce.9.cloned.1.call-start = ((), (), s32[]{:S(2)}) async-start(), calls=%async_computation.1 | async-start | bytes 262144 | tf_op jit(solution)/shard_map/psum | solution.py:24
  34.0 276.1 %copy-start.1 = (f32[128,4096]{1,0:T(8,128)}, f32[128,4096]{1,0:T(8,128)S(1)}, u32[]{:S(2)}) copy-start(f32[128,4096]{1,0:T(8,128)S(1)} %convert_element_type.15) | copy-start | bytes 6291460
  66.8 242.4 %all-reduce.11.cloned.1.call-start = ((), (), s32[]{:S(2)}) async-start(), calls=%async_computation.2 | async-start | bytes 131072 | tf_op jit(solution)/shard_map/psum | solution.py:24
  136.0 78.4 %copy-start.2 = (f32[8,4096]{1,0:T(8,128)S(1)}, f32[8,4096]{1,0:T(8,128)}, u32[]{:S(2)}) copy-start(f32[8,4096]{1,0:T(8,128)} %all-reduce.9.cloned.1.call-done) | copy-start | bytes 393220
  240.7 74.4 %copy-start.4 = (f32[256]{0:T(256)S(1)}, f32[256]{0:T(256)}, u32[]{:S(2)}) copy-start(f32[256]{0:T(256)} %param.11) | copy-start | bytes 3076
  240.7 74.4 %copy-start.5 = (f32[128]{0:T(128)S(1)}, f32[128]{0:T(128)}, u32[]{:S(2)}) copy-start(f32[128]{0:T(128)} %param.10) | copy-start | bytes 1540
  240.7 112.1 %copy-start = (f32[4,128,256]{2,1,0:T(8,128)S(1)}, f32[4,128,256]{2,1,0:T(8,128)}, u32[]{:S(2)}) copy-start(f32[4,128,256]{2,1,0:T(8,128)} %param.6) | copy-start | bytes 1572868
  240.8 110.7 %all-reduce.13.cloned.1.call-start = ((), (), s32[]{:S(2)}) async-start(), calls=%async_computation.3 | async-start | bytes 2097152 | tf_op jit(solution)/shard_map/psum | solution.py:27
  315.1 132.9 %all-reduce.15.cloned.1.call-start = ((), (), s32[]{:S(2)}) async-start(), calls=%async_computation.4 | async-start | bytes 262144 | tf_op jit(solution)/shard_map/psum | solution.py:24
  380.5 240.7 %all-reduce.17.cloned.1.call-start = ((), (), s32[]{:S(2)}) async-start(), calls=%async_computation.5 | async-start | bytes 131072 | tf_op jit(solution)/shard_map/psum | solution.py:24
  448.0 78.4 %copy-start.3 = (f32[8,4096]{1,0:T(8,128)S(1)}, f32[8,4096]{1,0:T(8,128)}, u32[]{:S(2)}) copy-start(f32[8,4096]{1,0:T(8,128)} %all-reduce.15.cloned.1.call-done) | copy-start | bytes 393220
  552.7 111.3 %all-reduce.19.cloned.1.call-start = ((), (), s32[]{:S(2)}) async-start(), calls=%async_computation.6 | async-start | bytes 2097152 | tf_op jit(solution)/shard_map/psum | solution.py:27
Sparse Core Ops, SparseCore 0:
  10.1 52.0 all-gather.1
  66.9 69.0 all-reduce.8
  240.9 68.2 all-reduce.10
  315.2 36.2 all-reduce.12
  380.6 67.3 all-reduce.14
  552.8 68.2 all-reduce.16
  627.7 36.2 all-reduce.18
where the time goes:
time: 700 us; the launch traced here: 697 us
  waiting for transfers between devices  373 us (53%)
  blocking collectives  161 us (23%)
  matrix products  135 us (19%)
  between operations  14.5 us (2%)
  other arithmetic  11.4 us (2%)
    psum x4, waiting for transfers between devices, row_total(): return lax.psum(values, 'row')  273 us
    dot_general x2, matrix products, shards(): jnp.einsum('bn,mn->bm', right_coeff, kernel, precision=lax.Precision.HIGH...  74.6 us
    psum x2, waiting for transfers between devices, col_total(): return lax.psum(values, 'col')  72.6 us
    psum x3, blocking collectives, row_total(): return lax.psum(values, 'row')  66.6 us
    all_gather x2, blocking collectives, shards(): right_all = lax.all_gather(right_zed, 'row', axis=1, tiled=True)  61.6 us
    dot_general x2, matrix products, shards(): jnp.einsum('bm,mn->bn', left_rows, kernel, precision=lax.Precision.HIGHES...  40.3 us
    all_gather x1, waiting for transfers between devices, shards(): panel = lax.all_gather(val_orb, 'row', axis=0, tiled=True)  26.6 us
    psum x2, blocking collectives, col_total(): return lax.psum(values, 'col')  20.5 us
  transfers between devices with their start and end apart: 7, of which 7 were waited for; matrix products, arithmetic and copies ran while one was open for 1% of the time, Pallas kernels for 0%

commit v1 on v0

--- a/solution.py
+++ b/solution.py
@@ -1,6 +1,10 @@
+import functools
+
 import jax
 import jax.numpy as jnp
 from jax import lax
+from jax.experimental import pallas as pl
+from jax.experimental.pallas import tpu as pltpu
 from jax.sharding import PartitionSpec as P
 
 ITERS = 2
@@ -136,6 +140,564 @@
     return (joined[:count], joined[count:], jnp.stack(record, axis=1))
 
 
+MESH = pl.DeviceIdType.MESH
+TERMS = 24
+ROWS_K = 256
+
+
+def fits(mesh, start_vec, cond_orb, val_orb, kernel, cond_energy, val_energy):
+    R, C = mesh.shape["row"], mesh.shape["col"]
+    points = kernel.shape[0]
+    chunk = points // (R * C)
+    local = cond_orb.shape[0] // R
+    kernel_bytes = 2 * (points // R) * (points // C)
+    return (
+        start_vec.shape[0] == 4
+        and R % 2 == 0
+        and C == 4
+        and chunk % ROWS_K == 0
+        and local % 32 == 0
+        and (val_orb.shape[0] // R) % 16 == 0
+        and val_orb.shape[0] == 256
+        and kernel_bytes <= 16 * 2**20
+    )
+
+
+def body_kernel(
+    R, C,
+    start, cond, val, kmat, energy,
+    out_r, out_l, out_c,
+    panel, kb, kf, xs, xb, img, wbuf, lhs_r, lhs_l, lacc, terms,
+    a_send, a_recv, b_row, b_left, c_rsend, c_rrecv, c_lsend, c_lrecv, d_row,
+    e_send, e_recv, y_all, g_all, t_all,
+    k_sem, p_up, p_dn, p_x, p_recv,
+    a_ss, a_rs, b_ss, b_rs, bl_ss, bl_rs, cr_ss, cr_rs, cl_ss, cl_rs, d_ss, d_rs,
+    e_ss, e_rs, y_ss, y_rs, g_ss, g_rs, t_ss, t_rs,
+):
+    row = lax.axis_index("row")
+    col = lax.axis_index("col")
+    count = start.shape[0]
+    stack = 2 * count
+    nc = start.shape[1]
+    nv = start.shape[2]
+    half = nc // 2
+    chunk = a_send.shape[-1]
+    span_row = kb.shape[0]
+    span_col = kb.shape[1]
+    Y = C // 2
+    core = lax.rem(col, 2)
+    ypos = col // 2
+    mate = ypos * 2 + 1 - core
+    f32, bf16 = jnp.float32, jnp.bfloat16
+    mine = col * R + row
+    owner_row = mine // C
+    slot_left = lax.rem(mine, C)
+
+    def remote(src, dst, ss, rs, to_row, to_col):
+        return pltpu.make_async_remote_copy(
+            src_ref=src, dst_ref=dst, send_sem=ss, recv_sem=rs,
+            device_id=(to_row, to_col), device_id_type=MESH,
+        )
+
+    def away(k):
+        return lax.rem(row + k, R)
+
+    barrier = pltpu.get_barrier_semaphore()
+
+    @pl.loop(1, R * C)
+    def _(k):
+        flat = lax.rem(row * C + col + k, R * C)
+        pl.semaphore_signal(barrier, inc=1, device_id=(flat // C, lax.rem(flat, C)), device_id_type=MESH)
+
+    def kcopy(i, slot):
+        return pltpu.make_async_copy(
+            kmat.at[pl.ds(i * ROWS_K, ROWS_K), :], kf.at[slot], k_sem.at[slot]
+        )
+
+    kcopy(0, 0).start()
+    kcopy(1, 1).start()
+    panel[row] = val[...]
+
+    for b in range(count):
+        sq = jnp.sum(start[b] * start[b], axis=0, keepdims=True)
+        terms[b, 0:1, :] = sq[:, :128] + sq[:, 128:]
+    lane = lax.broadcasted_iota(jnp.int32, (8, 128), 1)
+    tile = jnp.zeros((8, 128), f32)
+    for b in range(count):
+        total = jnp.sum(terms[b, 0:1, :], axis=1, keepdims=True)
+        tile = tile + jnp.where(lane == b, total, 0.0)
+    t_all[0, row, 0:8, :] = tile
+    t_all[0, row, 8:TERMS, :] = jnp.zeros((TERMS - 8, 128), f32)
+
+    pl.semaphore_wait(barrier, R * C - 1)
+
+    def table_start(i):
+        @pl.loop(1, R)
+        def _(k):
+            peer = away(k)
+            remote(t_all.at[i, row], t_all.at[i, row], t_ss.at[i, peer], t_rs.at[i, row], peer, col).start()
+
+    def table_wait(i):
+        @pl.loop(1, R)
+        def _(k):
+            peer = away(k)
+            remote(t_all.at[i, row], t_all.at[i, peer], t_ss.at[i, peer], t_rs.at[i, peer], peer, col).wait_recv()
+        total = t_all[i, 0]
+        for k in range(1, R):
+            total = total + t_all[i, k]
+        return total
+
+    table_start(0)
+
+    L = R // 2
+    line = row // 2
+    side = lax.rem(row, 2)
+    pair = line * 2 + 1 - side
+
+    def blk(block, sem, to_row):
+        return remote(panel.at[block], panel.at[block], sem.at[block], p_recv.at[block], to_row, col)
+
+    def pass_on(block, up, down):
+        if up:
+            @pl.when(line + 1 < L)
+            def _():
+                blk(block, p_up, row + 2).start()
+        if down:
+            @pl.when(line >= 1)
+            def _():
+                blk(block, p_dn, row - 2).start()
+        blk(block, p_x, pair).start()
+
+    pass_on(row, True, True)
+
+    n_k = span_row // ROWS_K
+
+    def take_k(i):
+        slot = lax.rem(i, 2)
+        kcopy(i, slot).wait()
+        base = pl.multiple_of(i * ROWS_K, ROWS_K)
+
+        @pl.loop(0, ROWS_K // 16)
+        def _(g):
+            at = pl.multiple_of(g * 16, 16)
+            kb[pl.ds(pl.multiple_of(base + at, 16), 16), :] = kf[slot, pl.ds(at, 16), :].astype(bf16)
+
+        @pl.when(i + 2 < n_k)
+        def _():
+            kcopy(i + 2, slot).start()
+
+    per = n_k // L
+    for d in range(L):
+        @pl.loop(d * per, n_k if d == L - 1 else (d + 1) * per)
+        def _(i):
+            take_k(i)
+        if d == 0:
+            total = table_wait(0)
+            scale = 1.0 / jnp.sqrt(total[0:1, :])
+            for b in range(count):
+                q = start[b] * scale[:, b:b + 1]
+                xs[0, b] = q
+                xs[0, count + b] = q
+                xb[b] = q.astype(bf16)
+        if d + 1 < L:
+            @pl.when(line - (d + 1) >= 0)
+            def _():
+                block = row - 2 * (d + 1)
+                blk(block, p_x, pair).wait_recv()
+                pass_on(block, True, False)
+
+            @pl.when(line + (d + 1) < L)
+            def _():
+                block = row + 2 * (d + 1)
+                blk(block, p_x, pair).wait_recv()
+                pass_on(block, False, True)
+
+    @pl.loop(0, L)
+    def _(z):
+        blk(z * 2 + 1 - side, p_x, pair).wait_recv()
+
+    for it in range(ITERS):
+        wide = count if it == 0 else stack
+
+        @pl.loop(1, R + 1)
+        def _(k):
+            peer = away(k)
+            at = pl.multiple_of(peer * chunk, chunk)
+            block = panel[:, :, pl.ds(at, chunk)].reshape(nv, chunk)
+            weight = cond[:, pl.ds(at, chunk)].astype(f32)
+            for b in range(wide):
+                paired = jnp.dot(xb[b], block, preferred_element_type=f32)
+                value = jnp.sum(paired * weight, axis=0, keepdims=True)
+                a_send[it, peer, b:b + 1, :] = value
+                if wide == count:
+                    a_send[it, peer, count + b:count + b + 1, :] = value
+
+            @pl.when(k < R)
+            def _():
+                remote(a_send.at[it, peer], a_recv.at[it, row], a_ss.at[it, peer], a_rs.at[it, row], peer, col).start()
+
+        @pl.loop(1, R)
+        def _(k):
+            peer = away(k)
+            remote(a_send.at[it, peer], a_recv.at[it, peer], a_ss.at[it, peer], a_rs.at[it, peer], peer, col).wait_recv()
+        a_recv[it, row] = a_send[it, row]
+        coeff = a_recv[it, 0]
+        for k in range(1, R):
+            coeff = coeff + a_recv[it, k]
+
+        b_row[it, row] = coeff
+        for j in range(C):
+            here = jnp.logical_and(owner_row == row, col == j)
+
+            @pl.when(here)
+            def _():
+                b_left[it, slot_left] = coeff
+
+            @pl.when(jnp.logical_not(here))
+            def _():
+                remote(b_row.at[it, row], b_left.at[it, slot_left], bl_ss.at[it, j], bl_rs.at[it, slot_left], owner_row, j).start()
+
+        @pl.loop(1, R)
+        def _(k):
+            peer = away(k)
+            remote(b_row.at[it, row], b_row.at[it, row], b_ss.at[it, peer], b_rs.at[it, row], peer, col).start()
+
+        def split(ref, dst, pieces):
+            for j in range(pieces):
+                piece = ref[it, j]
+                high = piece.astype(bf16)
+                low = (piece - high.astype(f32)).astype(bf16)
+                dst[:, j * chunk:(j + 1) * chunk] = jnp.concatenate([high, low], axis=0)
+
+        @pl.loop(1, R)
+        def _(k):
+            peer = away(k)
+            remote(b_row.at[it, row], b_row.at[it, peer], b_ss.at[it, peer], b_rs.at[it, peer], peer, col).wait_recv()
+        split(b_row, lhs_r, R)
+
+        for s in range(C):
+            g = row * C + s
+            own_row, own_col = lax.rem(g, R), g // R
+            here = jnp.logical_and(own_row == row, own_col == col)
+
+            @pl.when(jnp.logical_not(here))
+            def _():
+                remote(b_row.at[it, row], b_left.at[it, s], bl_ss.at[it, s], bl_rs.at[it, s], own_row, own_col).wait_recv()
+        split(b_left, lhs_l, C)
+
+        lacc[...] = jnp.zeros_like(lacc)
+
+        @pl.loop(0, C)
+        def _(s):
+            g = row * C + s
+            own_row, own_col = lax.rem(g, R), g // R
+            at = pl.multiple_of(s * chunk, chunk)
+            part = kb[pl.ds(at, chunk), :]
+            right = lax.dot_general(lhs_r[...], part, (((1,), (1,)), ((), ())), preferred_element_type=f32)
+            c_rsend[it, s] = right[:8] + right[8:]
+            here = jnp.logical_and(own_row == row, own_col == col)
+
+            @pl.when(here)
+            def _():
+                c_rrecv[it, col] = c_rsend[it, s]
+
+            @pl.when(jnp.logical_not(here))
+            def _():
+                remote(c_rsend.at[it, s], c_rrecv.at[it, col], cr_ss.at[it, s], cr_rs.at[it, col], own_row, own_col).start()
+            left = jnp.dot(lhs_l[:, pl.ds(at, chunk)], part, preferred_element_type=f32)
+            lacc[...] += left[:8] + left[8:]
+
+        for j in range(R):
+            c_lsend[it, j] = lacc[:, j * chunk:(j + 1) * chunk]
+        c_lrecv[it, row] = c_lsend[it, row]
+
+        @pl.loop(1, R)
+        def _(k):
+            peer = away(k)
+            remote(c_lsend.at[it, peer], c_lrecv.at[it, row], cl_ss.at[it, peer], cl_rs.at[it, row], peer, col).start()
+
+        for j in range(C):
+            here = jnp.logical_and(owner_row == row, col == j)
+
+            @pl.when(jnp.logical_not(here))
+            def _():
+                remote(c_rsend.at[it, j], c_rrecv.at[it, j], cr_ss.at[it, j], cr_rs.at[it, j], owner_row, j).wait_recv()
+
+        @pl.loop(1, R)
+        def _(k):
+            peer = away(k)
+            remote(c_lsend.at[it, peer], c_lrecv.at[it, peer], cl_ss.at[it, peer], cl_rs.at[it, peer], peer, col).wait_recv()
+        zr = c_rrecv[it, 0]
+        for j in range(1, C):
+            zr = zr + c_rrecv[it, j]
+        zl = c_lrecv[it, 0]
+        for j in range(1, R):
+            zl = zl + c_lrecv[it, j]
+        sub = lax.broadcasted_iota(jnp.int32, (stack, chunk), 0)
+        d_row[it, row] = jnp.where(sub < count, zr, zl)
+
+        @pl.loop(1, R)
+        def _(k):
+            peer = away(k)
+            remote(d_row.at[it, row], d_row.at[it, row], d_ss.at[it, peer], d_rs.at[it, row], peer, col).start()
+
+        @pl.loop(1, R)
+        def _(k):
+            peer = away(k)
+            remote(d_row.at[it, row], d_row.at[it, peer], d_ss.at[it, peer], d_rs.at[it, peer], peer, col).wait_recv()
+
+        def e_copy(b):
+            return remote(e_send.at[it, b], e_recv.at[it, b], e_ss.at[it, b], e_rs.at[it, b], row, mate)
+
+        def y_copy(b, k, sender):
+            other = lax.rem(ypos + k, Y)
+            return remote(
+                y_all.at[it, ypos, b], y_all.at[it, sender, b], y_ss.at[it, k, b], y_rs.at[it, sender, b],
+                row, other * 2 + core,
+            )
+
+        def g_copy(b, sender):
+            return remote(g_all.at[it, core, b], g_all.at[it, sender, b], g_ss.at[it, b], g_rs.at[it, sender, b], row, mate)
+
+        own = pl.ds(pl.multiple_of(core * half, half), half)
+        rest = pl.ds(pl.multiple_of((1 - core) * half, half), half)
+
+        def backward(b):
+            for j in range(R):
+                at = slice(j * chunk, (j + 1) * chunk)
+                z = d_row[it, j, pl.ds(b, 1), :]
+                wbuf[:, at] = (cond[:, at].astype(f32) * z).astype(bf16)
+            total = jnp.zeros((nc, nv), f32)
+            for j in range(R):
+                at = slice(j * chunk, (j + 1) * chunk)
+                total = total + lax.dot_general(
+                    wbuf[:, at], panel[:, :, at].reshape(nv, chunk), (((1,), (1,)), ((), ())),
+                    preferred_element_type=f32,
+                )
+            img[b] = total
+            e_send[it, b] = img[b, rest, :].astype(bf16)
+            e_copy(b).start()
+
+        def cross(b):
+            e_copy(b).wait_recv()
+            y_all[it, ypos, b] = (img[b, own, :] + e_recv[it, b].astype(f32)).astype(bf16)
+            for k in range(1, Y):
+                y_copy(b, k, ypos).start()
+
+        def finish(b):
+            for k in range(1, Y):
+                y_copy(b, k, lax.rem(ypos + k, Y)).wait_recv()
+            total = y_all[it, 0, b].astype(f32)
+            for k in range(1, Y):
+                total = total + y_all[it, k, b].astype(f32)
+            g_all[it, core, b] = total.astype(bf16)
+            g_copy(b, core).start()
+
+        @pl.loop(0, stack)
+        def _(b):
+            backward(b)
+
+            @pl.when(b >= 1)
+            def _():
+                cross(b - 1)
+
+        cross(stack - 1)
+
+        @pl.loop(0, stack)
+        def _(b):
+            finish(b)
+
+        @pl.loop(0, stack)
+        def _(b):
+            g_copy(b, 1 - core).wait_recv()
+            for h in range(2):
+                rows = slice(h * half, (h + 1) * half)
+                img[b, rows, :] = energy[rows, :] * xs[it, b, rows, :] + g_all[it, h, b].astype(f32)
+
+        for b in range(count):
+            def add(g, acc):
+                at = pl.ds(pl.multiple_of(g * 8, 8), 8)
+                ir, il = img[b, at, :], img[count + b, at, :]
+                q, p = xs[it, b, at, :], xs[it, count + b, at, :]
+                if it == 0:
+                    pairs = [(p, ir), (il, ir), (il, q), (p, q), (ir, ir), (q, q), (ir, q), (il, il), (p, p), (il, p)]
+                else:
+                    qo, po = xs[it - 1, b, at, :], xs[it - 1, count + b, at, :]
+                    pairs = [
+                        (p, ir), (il, ir), (il, q), (p, q), (ir, ir), (q, q), (ir, q), (il, il), (p, p), (il, p),
+                        (po, ir), (qo, il), (p, qo), (po, q), (po, qo), (qo, qo), (ir, qo), (q, qo), (po, po), (il, po), (p, po),
+                    ]
+                out = []
+                for old, (u, w) in zip(acc, pairs):
+                    prod = u * w
+                    out.append(old + prod[:, :128] + prod[:, 128:])
+                return tuple(out)
+            n_terms = 10 if it == 0 else 21
+            acc = lax.fori_loop(0, nc // 8, add, tuple(jnp.zeros((8, 128), f32) for _ in range(n_terms)))
+            for t in range(n_terms):
+                terms[b, t:t + 1, :] = jnp.sum(acc[t], axis=0, keepdims=True)
+            terms[b, n_terms:TERMS, :] = jnp.zeros((TERMS - n_terms, 128), f32)
+        lanes = lax.broadcasted_iota(jnp.int32, (TERMS, 128), 1)
+        tile = jnp.zeros((TERMS, 128), f32)
+        for b in range(count):
+            tile = tile + jnp.where(lanes == b, jnp.sum(terms[b], axis=1, keepdims=True), 0.0)
+        t_all[it + 1, row] = tile
+        table_start(it + 1)
+        table = table_wait(it + 1)
+        T = [table[t:t + 1, :] for t in range(TERMS)]
+        alpha = T[0]
+        cross_term = T[1] - alpha * T[2] - alpha * alpha + alpha * alpha * T[3]
+        right_sq = T[4] + alpha * alpha * T[5] - 2.0 * alpha * T[6]
+        left_sq = T[7] + alpha * alpha * T[8] - 2.0 * alpha * T[9]
+        if it:
+            mu, nu = T[10], T[11]
+            cross_term = (
+                cross_term - mu * nu + alpha * mu * T[12] - nu * mu + nu * alpha * T[13] + nu * mu * T[14]
+            )
+            right_sq = right_sq + mu * mu * T[15] - 2.0 * mu * T[16] + 2.0 * alpha * mu * T[17]
+            left_sq = left_sq + nu * nu * T[18] - 2.0 * nu * T[19] + 2.0 * alpha * nu * T[20]
+        beta = jnp.sqrt(jnp.maximum(cross_term, 0.25 * jnp.sqrt(right_sq * left_sq)))
+        out_c[2 * it:2 * it + 1, :] = alpha
+        out_c[2 * it + 1:2 * it + 2, :] = beta
+        inverse = 1.0 / beta
+        for b in range(count):
+            one = slice(b, b + 1)
+            r = img[b] - alpha[:, one] * xs[it, b]
+            s = img[count + b] - alpha[:, one] * xs[it, count + b]
+            if it:
+                r = r - mu[:, one] * xs[it - 1, b]
+                s = s - nu[:, one] * xs[it - 1, count + b]
+            r = r * inverse[:, one]
+            s = s * inverse[:, one]
+            if it + 1 == ITERS:
+                out_r[b] = r
+                out_l[b] = s
+            else:
+                xs[it + 1, b] = r
+                xs[it + 1, count + b] = s
+                xb[b] = r.astype(bf16)
+                xb[count + b] = s.astype(bf16)
+
+        @pl.loop(1, R)
+        def _(k):
+            peer = away(k)
+            remote(a_send.at[it, peer], a_recv.at[it, row], a_ss.at[it, peer], a_rs.at[it, row], peer, col).wait_send()
+            remote(b_row.at[it, row], b_row.at[it, row], b_ss.at[it, peer], b_rs.at[it, row], peer, col).wait_send()
+            remote(c_lsend.at[it, peer], c_lrecv.at[it, row], cl_ss.at[it, peer], cl_rs.at[it, row], peer, col).wait_send()
+            remote(d_row.at[it, row], d_row.at[it, row], d_ss.at[it, peer], d_rs.at[it, row], peer, col).wait_send()
+            remote(t_all.at[it + 1, row], t_all.at[it + 1, row], t_ss.at[it + 1, peer], t_rs.at[it + 1, row], peer, col).wait_send()
+
+        for j in range(C):
+            here = jnp.logical_and(owner_row == row, col == j)
+
+            @pl.when(jnp.logical_not(here))
+            def _():
+                remote(b_row.at[it, row], b_left.at[it, slot_left], bl_ss.at[it, j], bl_rs.at[it, slot_left], owner_row, j).wait_send()
+
+            g = row * C + j
+            own_row, own_col = lax.rem(g, R), g // R
+            there = jnp.logical_and(own_row == row, own_col == col)
+
+            @pl.when(jnp.logical_not(there))
+            def _():
+                remote(c_rsend.at[it, j], c_rrecv.at[it, col], cr_ss.at[it, j], cr_rs.at[it, col], own_row, own_col).wait_send()
+
+        @pl.loop(0, stack)
+        def _(b):
+            e_copy(b).wait_send()
+            for k in range(1, Y):
+                y_copy(b, k, ypos).wait_send()
+            g_copy(b, core).wait_send()
+
+    @pl.loop(1, R)
+    def _(k):
+        peer = away(k)
+        remote(t_all.at[0, row], t_all.at[0, row], t_ss.at[0, peer], t_rs.at[0, row], peer, col).wait_send()
+
+    @pl.loop(0, L)
+    def _(z):
+        block = z * 2 + side
+        blk(block, p_x, pair).wait_send()
+
+        @pl.when(jnp.logical_and(z <= line, line + 1 < L))
+        def _():
+            blk(block, p_up, row + 2).wait_send()
+
+        @pl.when(jnp.logical_and(z >= line, line >= 1))
+        def _():
+            blk(block, p_dn, row - 2).wait_send()
+
+
+def fused(mesh, start_vec, cond_orb, val_orb, kernel, cond_energy, val_energy):
+    R, C = mesh.shape["row"], mesh.shape["col"]
+    count, nc, nv = start_vec.shape
+    stack = 2 * count
+    half = nc // 2
+    span_row, span_col = kernel.shape
+    vs = val_orb.shape[0]
+    chunk = span_row // C
+    Y = C // 2
+    f32, bf16 = jnp.float32, jnp.bfloat16
+    V = pltpu.VMEM
+    D = pltpu.SemaphoreType.DMA
+    energy = cond_energy[:, None] - val_energy[None, :]
+    vm = pl.BlockSpec(memory_space=pltpu.VMEM)
+    scratch = [
+        V((R, vs, span_col), bf16),
+        V((span_row, span_col), bf16),
+        V((2, ROWS_K, span_col), f32),
+        V((ITERS, stack, nc, nv), f32),
+        V((stack, nc, nv), bf16),
+        V((stack, nc, nv), f32),
+        V((nc, span_col), bf16),
+        V((2 * stack, span_col), bf16),
+        V((2 * stack, span_row), bf16),
+        V((stack, span_col), f32),
+        V((count, TERMS, 128), f32),
+        V((ITERS, R, stack, chunk), f32),
+        V((ITERS, R, stack, chunk), f32),
+        V((ITERS, R, stack, chunk), f32),
+        V((ITERS, C, stack, chunk), f32),
+        V((ITERS, C, stack, chunk), f32),
+        V((ITERS, C, stack, chunk), f32),
+        V((ITERS, R, stack, chunk), f32),
+        V((ITERS, R, stack, chunk), f32),
+        V((ITERS, R, stack, chunk), f32),
+        V((ITERS, stack, half, nv), bf16),
+        V((ITERS, stack, half, nv), bf16),
+        V((ITERS, Y, stack, half, nv), bf16),
+        V((ITERS, 2, stack, half, nv), bf16),
+        V((ITERS + 1, R, TERMS, 128), f32),
+        D((2,)),
+        D((R,)), D((R,)), D((R,)), D((R,)),
+        D((ITERS, R)), D((ITERS, R)),
+        D((ITERS, R)), D((ITERS, R)),
+        D((ITERS, C)), D((ITERS, C)),
+        D((ITERS, C)), D((ITERS, C)),
+        D((ITERS, R)), D((ITERS, R)),
+        D((ITERS, R)), D((ITERS, R)),
+        D((ITERS, stack)), D((ITERS, stack)),
+        D((ITERS, Y, stack)), D((ITERS, Y, stack)),
+        D((ITERS, stack)), D((ITERS, 2, stack)),
+        D((ITERS + 1, R)), D((ITERS + 1, R)),
+    ]
+    right, left, coefs = pl.pallas_call(
+        functools.partial(body_kernel, R, C),
+        out_shape=(
+            jax.ShapeDtypeStruct((count, nc, nv), f32),
+            jax.ShapeDtypeStruct((count, nc, nv), f32),
+            jax.ShapeDtypeStruct((2 * ITERS, 128), f32),
+        ),
+        in_specs=[vm, vm, vm, pl.BlockSpec(memory_space=pl.ANY), vm],
+        out_specs=(vm, vm, vm),
+        scratch_shapes=scratch,
+        compiler_params=pltpu.CompilerParams(
+            collective_id=0, has_side_effects=True, vmem_limit_bytes=62 * 2**20
+        ),
+    )(start_vec, cond_orb, val_orb, kernel, energy)
+    return right, left, coefs[:, :count].T
+
+
 def solution(mesh):
     in_specs = (
         P(None, "row", None),
@@ -146,4 +708,15 @@
         P(),
     )
     out_specs = (P(None, "row", None), P(None, "row", None), P())
-    return jax.shard_map(shards, mesh=mesh, in_specs=in_specs, out_specs=out_specs, check_vma=False)
+
+    def run(*arrays):
+        body = fused if fits(mesh, *arrays) else shards
+        return jax.shard_map(
+            functools.partial(body, mesh) if body is fused else body,
+            mesh=mesh,
+            in_specs=in_specs,
+            out_specs=out_specs,
+            check_vma=False,
+        )(*arrays)
+
+    return run

time: 700 us -> 143 us (0.20)
  waiting for transfers between devices: 373 us -> 0 us
  blocking collectives: 161 us -> 0 us
  Pallas kernels: 0 us -> 136 us
  matrix products: 135 us -> 0 us
  between operations: 14.5 us -> 0.64 us
  other arithmetic: 11.4 us -> 1.42 us
    psum x6 -> x0, waiting for transfers between devices: 345 us -> none  [the longest x4 273 us: row_total(): return lax.psum(values, 'row')]
    pallas_call x0 -> x1, Pallas kernels: none -> 136 us  [fused(): pl.pallas_call(functools.partial(body_kernel, R, C), out_shape=(jax.Shape...]
    dot_general x8 -> x0, matrix products: 135 us -> none  [the longest x2 74.6 us: shards(): jnp.einsum('bn,mn->bm', right_coeff, kernel, precision=lax.Precision.HIGH...]
    psum x5 -> x0, blocking collectives: 87.1 us -> none  [the longest x3 66.6 us: row_total(): return lax.psum(values, 'row')]
    all_gather x4 -> x0, blocking collectives: 73.9 us -> none  [the longest x2 61.6 us: shards(): right_all = lax.all_gather(right_zed, 'row', axis=1, tiled=True)]
    all_gather x1 -> x0, waiting for transfers between devices: 26.6 us -> none  [shards(): panel = lax.all_gather(val_orb, 'row', axis=0, tiled=True)]
  transfers between devices with their start and end apart: 7 -> 0, of which waited for: 7 -> 0; matrix products, arithmetic and copies ran while one was open for 1% -> 0% of each run, Pallas kernels for 0% -> 0%
where the time goes in v1:
time: 143 us
  Pallas kernels  136 us (95%)
  local copies, waits for them, and re-layouts  5.08 us (4%)
    pallas_call x1, Pallas kernels, fused(): pl.pallas_call(functools.partial(body_kernel, R, C), out_shape=(jax.Shape...  136 us
    unnamed x3, local copies, waits for them, and re-layouts  4.4 us

profile of v1, /device:TPU:0, one launch (start us, length us, event | category | flops | bytes accessed | tf_op | source)
XLA Modules:
  0.0 142.9 jit_solution(1822203889244746340)
XLA Ops:
  0.6 1.4 broadcast_subtract_fusion.energy
  2.1 135.8 %shard_map.85 = (f32[4,128,256]{2,1,0:T(8,128)}, f32[4,128,256]{2,1,0:T(8,128)}, f32[4,128]{1,0:T(4,128)}) custom-call(f32[4,128,256]{2,1,0:T(8,128)} %start.1, bf16[128,4096]{1,0:T(8,128)(2,1)} %cond.1, bf16[32,4096]{1,0:T(8,128)(2,1)} %val.1, f32[2048,4096]{1,0:T(8,128)} %kmat.1, f32[128,256]{1,0:T(8,128)} %broadcast_subtract_fusion.energy), custom_call_target="tpu_custom_call" | custom-call | tf_op jit(solution)/shard_map/pallas_call | solution.py:684
  137.9 0.7 slice_bitcast_fusion
  138.5 0.7 copy.9
  139.2 1.9 %copy.12 = f32[4,128,256]{2,1,0:T(8,128)} copy(f32[4,128,256]{2,1,0:T(8,128)} %get-tuple-element.15) | data formatting | bytes 1048576
  141.1 1.9 %copy.13 = f32[4,128,256]{2,1,0:T(8,128)} copy(f32[4,128,256]{2,1,0:T(8,128)} %get-tuple-element.16) | data formatting | bytes 1048576

commit v2 on v1

--- a/solution.py
+++ b/solution.py
@@ -167,8 +167,8 @@
     R, C,
     start, cond, val, kmat, energy,
     out_r, out_l, out_c,
-    panel, kb, kf, xs, xb, img, wbuf, lhs_r, lhs_l, lacc, terms,
-    a_send, a_recv, b_row, b_left, c_rsend, c_rrecv, c_lsend, c_lrecv, d_row,
+    panel, kb, kf, xs, xb, img, wbuf, lhs_r, lhs_l, terms,
+    a0_send, a0_recv, a1_send, a1_recv, b_row, b_own, b_left, c_rsend, c_rrecv, c_lsend, c_lrecv, d_row,
     e_send, e_recv, y_all, g_all, t_all,
     k_sem, p_up, p_dn, p_x, p_recv,
     a_ss, a_rs, b_ss, b_rs, bl_ss, bl_rs, cr_ss, cr_rs, cl_ss, cl_rs, d_ss, d_rs,
@@ -181,7 +181,7 @@
     nc = start.shape[1]
     nv = start.shape[2]
     half = nc // 2
-    chunk = a_send.shape[-1]
+    chunk = a0_send.shape[-1]
     span_row = kb.shape[0]
     span_col = kb.shape[1]
     Y = C // 2
@@ -226,8 +226,7 @@
     for b in range(count):
         total = jnp.sum(terms[b, 0:1, :], axis=1, keepdims=True)
         tile = tile + jnp.where(lane == b, total, 0.0)
-    t_all[0, row, 0:8, :] = tile
-    t_all[0, row, 8:TERMS, :] = jnp.zeros((TERMS - 8, 128), f32)
+    t_all[0, row] = tile
 
     pl.semaphore_wait(barrier, R * C - 1)
 
@@ -318,6 +317,7 @@
 
     for it in range(ITERS):
         wide = count if it == 0 else stack
+        a_send, a_recv = (a0_send, a0_recv) if it == 0 else (a1_send, a1_recv)
 
         @pl.loop(1, R + 1)
         def _(k):
@@ -328,34 +328,35 @@
             for b in range(wide):
                 paired = jnp.dot(xb[b], block, preferred_element_type=f32)
                 value = jnp.sum(paired * weight, axis=0, keepdims=True)
-                a_send[it, peer, b:b + 1, :] = value
-                if wide == count:
-                    a_send[it, peer, count + b:count + b + 1, :] = value
+                a_send[peer, b:b + 1, :] = value
 
             @pl.when(k < R)
             def _():
-                remote(a_send.at[it, peer], a_recv.at[it, row], a_ss.at[it, peer], a_rs.at[it, row], peer, col).start()
-
-        @pl.loop(1, R)
-        def _(k):
-            peer = away(k)
-            remote(a_send.at[it, peer], a_recv.at[it, peer], a_ss.at[it, peer], a_rs.at[it, peer], peer, col).wait_recv()
-        a_recv[it, row] = a_send[it, row]
-        coeff = a_recv[it, 0]
+                remote(a_send.at[peer], a_recv.at[row], a_ss.at[it, peer], a_rs.at[it, row], peer, col).start()
+
+        @pl.loop(1, R)
+        def _(k):
+            peer = away(k)
+            remote(a_send.at[peer], a_recv.at[peer], a_ss.at[it, peer], a_rs.at[it, peer], peer, col).wait_recv()
+        a_recv[row] = a_send[row]
+        coeff = a_recv[0]
         for k in range(1, R):
-            coeff = coeff + a_recv[it, k]
-
-        b_row[it, row] = coeff
+            coeff = coeff + a_recv[k]
+        right_coeff = coeff[:count]
+        left_coeff = coeff if it == 0 else coeff[count:]
+
+        b_row[it, row] = right_coeff
+        b_own[it] = left_coeff
         for j in range(C):
             here = jnp.logical_and(owner_row == row, col == j)
 
             @pl.when(here)
             def _():
-                b_left[it, slot_left] = coeff
+                b_left[it, slot_left] = left_coeff
 
             @pl.when(jnp.logical_not(here))
             def _():
-                remote(b_row.at[it, row], b_left.at[it, slot_left], bl_ss.at[it, j], bl_rs.at[it, slot_left], owner_row, j).start()
+                remote(b_own.at[it], b_left.at[it, slot_left], bl_ss.at[it, j], bl_rs.at[it, slot_left], owner_row, j).start()
 
         @pl.loop(1, R)
         def _(k):
@@ -365,15 +366,8 @@
         def split(ref, dst, pieces):
             for j in range(pieces):
                 piece = ref[it, j]
-                high = piece.astype(bf16)
-                low = (piece - high.astype(f32)).astype(bf16)
-                dst[:, j * chunk:(j + 1) * chunk] = jnp.concatenate([high, low], axis=0)
-
-        @pl.loop(1, R)
-        def _(k):
-            peer = away(k)
-            remote(b_row.at[it, row], b_row.at[it, peer], b_ss.at[it, peer], b_rs.at[it, peer], peer, col).wait_recv()
-        split(b_row, lhs_r, R)
+                high = piece.astype(bf16).astype(f32)
+                dst[:, j * chunk:(j + 1) * chunk] = jnp.concatenate([high, piece - high], axis=0).astype(bf16)
 
         for s in range(C):
             g = row * C + s
@@ -382,19 +376,35 @@
 
             @pl.when(jnp.logical_not(here))
             def _():
-                remote(b_row.at[it, row], b_left.at[it, s], bl_ss.at[it, s], bl_rs.at[it, s], own_row, own_col).wait_recv()
+                remote(b_own.at[it], b_left.at[it, s], bl_ss.at[it, s], bl_rs.at[it, s], own_row, own_col).wait_recv()
         split(b_left, lhs_l, C)
 
-        lacc[...] = jnp.zeros_like(lacc)
+        @pl.loop(1, R + 1)
+        def _(k):
+            peer = away(k)
+            at = pl.multiple_of(peer * chunk, chunk)
+            left = jnp.dot(lhs_l[...], kb[:, pl.ds(at, chunk)], preferred_element_type=f32)
+            c_lsend[it, peer] = left[:count] + left[count:]
+
+            @pl.when(k < R)
+            def _():
+                remote(c_lsend.at[it, peer], c_lrecv.at[it, row], cl_ss.at[it, peer], cl_rs.at[it, row], peer, col).start()
+
+        c_lrecv[it, row] = c_lsend[it, row]
+
+        @pl.loop(1, R)
+        def _(k):
+            peer = away(k)
+            remote(b_row.at[it, row], b_row.at[it, peer], b_ss.at[it, peer], b_rs.at[it, peer], peer, col).wait_recv()
+        split(b_row, lhs_r, R)
 
         @pl.loop(0, C)
         def _(s):
             g = row * C + s
             own_row, own_col = lax.rem(g, R), g // R
-            at = pl.multiple_of(s * chunk, chunk)
-            part = kb[pl.ds(at, chunk), :]
+            part = kb[pl.ds(pl.multiple_of(s * chunk, chunk), chunk), :]
             right = lax.dot_general(lhs_r[...], part, (((1,), (1,)), ((), ())), preferred_element_type=f32)
-            c_rsend[it, s] = right[:8] + right[8:]
+            c_rsend[it, s] = right[:count] + right[count:]
             here = jnp.logical_and(own_row == row, own_col == col)
 
             @pl.when(here)
@@ -404,17 +414,6 @@
             @pl.when(jnp.logical_not(here))
             def _():
                 remote(c_rsend.at[it, s], c_rrecv.at[it, col], cr_ss.at[it, s], cr_rs.at[it, col], own_row, own_col).start()
-            left = jnp.dot(lhs_l[:, pl.ds(at, chunk)], part, preferred_element_type=f32)
-            lacc[...] += left[:8] + left[8:]
-
-        for j in range(R):
-            c_lsend[it, j] = lacc[:, j * chunk:(j + 1) * chunk]
-        c_lrecv[it, row] = c_lsend[it, row]
-
-        @pl.loop(1, R)
-        def _(k):
-            peer = away(k)
-            remote(c_lsend.at[it, peer], c_lrecv.at[it, row], cl_ss.at[it, peer], cl_rs.at[it, row], peer, col).start()
 
         for j in range(C):
             here = jnp.logical_and(owner_row == row, col == j)
@@ -433,8 +432,7 @@
         zl = c_lrecv[it, 0]
         for j in range(1, R):
             zl = zl + c_lrecv[it, j]
-        sub = lax.broadcasted_iota(jnp.int32, (stack, chunk), 0)
-        d_row[it, row] = jnp.where(sub < count, zr, zl)
+        d_row[it, row] = jnp.concatenate([zr, zl], axis=0)
 
         @pl.loop(1, R)
         def _(k):
@@ -475,12 +473,12 @@
                     preferred_element_type=f32,
                 )
             img[b] = total
-            e_send[it, b] = img[b, rest, :].astype(bf16)
+            e_send[it, b] = img[b, rest, :]
             e_copy(b).start()
 
         def cross(b):
             e_copy(b).wait_recv()
-            y_all[it, ypos, b] = (img[b, own, :] + e_recv[it, b].astype(f32)).astype(bf16)
+            y_all[it, ypos, b] = (img[b, own, :] + e_recv[it, b]).astype(bf16)
             for k in range(1, Y):
                 y_copy(b, k, ypos).start()
 
@@ -490,7 +488,7 @@
             total = y_all[it, 0, b].astype(f32)
             for k in range(1, Y):
                 total = total + y_all[it, k, b].astype(f32)
-            g_all[it, core, b] = total.astype(bf16)
+            g_all[it, core, b] = total
             g_copy(b, core).start()
 
         @pl.loop(0, stack)
@@ -512,7 +510,7 @@
             g_copy(b, 1 - core).wait_recv()
             for h in range(2):
                 rows = slice(h * half, (h + 1) * half)
-                img[b, rows, :] = energy[rows, :] * xs[it, b, rows, :] + g_all[it, h, b].astype(f32)
+                img[b, rows, :] = energy[rows, :] * xs[it, b, rows, :] + g_all[it, h, b]
 
         for b in range(count):
             def add(g, acc):
@@ -520,7 +518,7 @@
                 ir, il = img[b, at, :], img[count + b, at, :]
                 q, p = xs[it, b, at, :], xs[it, count + b, at, :]
                 if it == 0:
-                    pairs = [(p, ir), (il, ir), (il, q), (p, q), (ir, ir), (q, q), (ir, q), (il, il), (p, p), (il, p)]
+                    pairs = [(q, ir), (il, ir), (il, q), (q, q), (ir, ir), (il, il)]
                 else:
                     qo, po = xs[it - 1, b, at, :], xs[it - 1, count + b, at, :]
                     pairs = [
@@ -532,19 +530,24 @@
                     prod = u * w
                     out.append(old + prod[:, :128] + prod[:, 128:])
                 return tuple(out)
-            n_terms = 10 if it == 0 else 21
+            n_terms = 6 if it == 0 else 21
             acc = lax.fori_loop(0, nc // 8, add, tuple(jnp.zeros((8, 128), f32) for _ in range(n_terms)))
             for t in range(n_terms):
                 terms[b, t:t + 1, :] = jnp.sum(acc[t], axis=0, keepdims=True)
             terms[b, n_terms:TERMS, :] = jnp.zeros((TERMS - n_terms, 128), f32)
-        lanes = lax.broadcasted_iota(jnp.int32, (TERMS, 128), 1)
-        tile = jnp.zeros((TERMS, 128), f32)
+        tile = jnp.zeros((8, 128), f32)
+        groups = 1 if it == 0 else TERMS // 8
         for b in range(count):
-            tile = tile + jnp.where(lanes == b, jnp.sum(terms[b], axis=1, keepdims=True), 0.0)
+            sums = jnp.sum(terms[b], axis=1, keepdims=True)
+            for g in range(groups):
+                tile = tile + jnp.where(lane == count * g + b, sums[8 * g:8 * g + 8], 0.0)
         t_all[it + 1, row] = tile
         table_start(it + 1)
         table = table_wait(it + 1)
-        T = [table[t:t + 1, :] for t in range(TERMS)]
+        packs = [table] + [pltpu.roll(table, 128 - count * g, 1) for g in range(1, groups)]
+        T = [packs[t // 8][t % 8:t % 8 + 1, :] for t in range(8 * groups)]
+        if it == 0:
+            T = [T[0], T[1], T[2], T[3], T[4], T[3], T[0], T[5], T[3], T[2]]
         alpha = T[0]
         cross_term = T[1] - alpha * T[2] - alpha * alpha + alpha * alpha * T[3]
         right_sq = T[4] + alpha * alpha * T[5] - 2.0 * alpha * T[6]
@@ -567,12 +570,12 @@
             if it:
                 r = r - mu[:, one] * xs[it - 1, b]
                 s = s - nu[:, one] * xs[it - 1, count + b]
-            r = r * inverse[:, one]
-            s = s * inverse[:, one]
             if it + 1 == ITERS:
                 out_r[b] = r
                 out_l[b] = s
             else:
+                r = r * inverse[:, one]
+                s = s * inverse[:, one]
                 xs[it + 1, b] = r
                 xs[it + 1, count + b] = s
                 xb[b] = r.astype(bf16)
@@ -581,7 +584,7 @@
         @pl.loop(1, R)
         def _(k):
             peer = away(k)
-            remote(a_send.at[it, peer], a_recv.at[it, row], a_ss.at[it, peer], a_rs.at[it, row], peer, col).wait_send()
+            remote(a_send.at[peer], a_recv.at[row], a_ss.at[it, peer], a_rs.at[it, row], peer, col).wait_send()
             remote(b_row.at[it, row], b_row.at[it, row], b_ss.at[it, peer], b_rs.at[it, row], peer, col).wait_send()
             remote(c_lsend.at[it, peer], c_lrecv.at[it, row], cl_ss.at[it, peer], cl_rs.at[it, row], peer, col).wait_send()
             remote(d_row.at[it, row], d_row.at[it, row], d_ss.at[it, peer], d_rs.at[it, row], peer, col).wait_send()
@@ -592,7 +595,7 @@
 
             @pl.when(jnp.logical_not(here))
             def _():
-                remote(b_row.at[it, row], b_left.at[it, slot_left], bl_ss.at[it, j], bl_rs.at[it, slot_left], owner_row, j).wait_send()
+                remote(b_own.at[it], b_left.at[it, slot_left], bl_ss.at[it, j], bl_rs.at[it, slot_left], owner_row, j).wait_send()
 
             g = row * C + j
             own_row, own_col = lax.rem(g, R), g // R
@@ -650,24 +653,26 @@
         V((stack, nc, nv), bf16),
         V((stack, nc, nv), f32),
         V((nc, span_col), bf16),
-        V((2 * stack, span_col), bf16),
-        V((2 * stack, span_row), bf16),
-        V((stack, span_col), f32),
+        V((stack, span_col), bf16),
+        V((stack, span_row), bf16),
         V((count, TERMS, 128), f32),
+        V((R, count, chunk), f32),
+        V((R, count, chunk), f32),
+        V((R, stack, chunk), f32),
+        V((R, stack, chunk), f32),
+        V((ITERS, R, count, chunk), f32),
+        V((ITERS, count, chunk), f32),
+        V((ITERS, C, count, chunk), f32),
+        V((ITERS, C, count, chunk), f32),
+        V((ITERS, C, count, chunk), f32),
+        V((ITERS, R, count, chunk), f32),
+        V((ITERS, R, count, chunk), f32),
         V((ITERS, R, stack, chunk), f32),
-        V((ITERS, R, stack, chunk), f32),
-        V((ITERS, R, stack, chunk), f32),
-        V((ITERS, C, stack, chunk), f32),
-        V((ITERS, C, stack, chunk), f32),
-        V((ITERS, C, stack, chunk), f32),
-        V((ITERS, R, stack, chunk), f32),
-        V((ITERS, R, stack, chunk), f32),
-        V((ITERS, R, stack, chunk), f32),
-        V((ITERS, stack, half, nv), bf16),
-        V((ITERS, stack, half, nv), bf16),
+        V((ITERS, stack, half, nv), f32),
+        V((ITERS, stack, half, nv), f32),
         V((ITERS, Y, stack, half, nv), bf16),
-        V((ITERS, 2, stack, half, nv), bf16),
-        V((ITERS + 1, R, TERMS, 128), f32),
+        V((ITERS, 2, stack, half, nv), f32),
+        V((ITERS + 1, R, 8, 128), f32),
         D((2,)),
         D((R,)), D((R,)), D((R,)), D((R,)),
         D((ITERS, R)), D((ITERS, R)),
@@ -695,7 +700,9 @@
             collective_id=0, has_side_effects=True, vmem_limit_bytes=62 * 2**20
         ),
     )(start_vec, cond_orb, val_orb, kernel, energy)
-    return right, left, coefs[:, :count].T
+    coefs = coefs[:, :count].T
+    beta = coefs[:, -1][:, None, None]
+    return right / beta, left / beta, coefs
 
 
 def solution(mesh):

time: 143 us -> 133 us (0.930)
  Pallas kernels: 136 us -> 127 us
  local copies, waits for them, and re-layouts: 5.08 us -> 1.33 us
  other arithmetic: 1.42 us -> 3.76 us
    pallas_call x1, Pallas kernels: 136 us -> 127 us  [fused(): pl.pallas_call(functools.partial(body_kernel, R, C), out_shape=(jax.Shape...]
    unnamed x3 -> x1, local copies, waits for them, and re-layouts: 4.4 us -> 0.66 us
    div x0 -> x1, other arithmetic: none -> 2.34 us  [fused(): return (right / beta, left / beta, coefs)]
where the time goes in v2:
time: 133 us; the launch traced here: 132 us
  Pallas kernels  127 us (95%)
  other arithmetic  3.76 us (3%)
  local copies, waits for them, and re-layouts  1.33 us (1%)
    pallas_call x1, Pallas kernels, fused(): pl.pallas_call(functools.partial(body_kernel, R, C), out_shape=(jax.Shape...  127 us

profile of v2, /device:TPU:0, one launch (start us, length us, event | category | flops | bytes accessed | tf_op | source)
XLA Modules:
  0.0 132.4 jit_solution(392655511038044788)
XLA Ops:
  0.6 1.4 %broadcast_subtract_fusion.energy = f32[128,256]{1,0:T(8,128)} fusion(f32[256]{0:T(256)} %param.11, f32[128]{0:T(128)} %param.10), kind=kLoop, calls=%fused_computation.2 | loop fusion | flops 32768 | bytes 132608 | tf_op jit(solution)/shard_map/sub | solution.py:646
  2.1 126.7 %shard_map.85 = (f32[4,128,256]{2,1,0:T(8,128)}, f32[4,128,256]{2,1,0:T(8,128)}, f32[4,128]{1,0:T(4,128)}) custom-call(f32[4,128,256]{2,1,0:T(8,128)} %start.1, bf16[128,4096]{1,0:T(8,128)(2,1)} %cond.1, bf16[32,4096]{1,0:T(8,128)(2,1)} %val.1, f32[2048,4096]{1,0:T(8,128)} %kmat.1, f32[128,256]{1,0:T(8,128)} %broadcast_subtract_fusion.energy), custom_call_target="tpu_custom_call" | custom-call | tf_op jit(solution)/shard_map/pallas_call | solution.py:689
  128.8 0.7 slice_bitcast_fusion
  129.4 2.3 %broadcast_divide_fusion = (f32[4,128,256]{2,1,0:T(8,128)}, f32[4,128,256]{2,1,0:T(8,128)}) fusion(f32[4,128,256]{2,1,0:T(8,128)} %get-tuple-element.8, f32[4]{0:T(128)S(1)} %slice_bitcast_fusion.1, f32[4,128,256]{2,1,0:T(8,128)} %get-tuple-element.6), kind=kLoop, calls=%fused_computation | loop fusion | flops 262144 | bytes 2097168 | tf_op jit(solution)/shard_map/div | solution.py:705
  131.8 0.7 copy.9
  (1 shorter events, 0.0 us)

commit v3 on v2

--- a/solution.py
+++ b/solution.py
@@ -168,10 +168,10 @@
     start, cond, val, kmat, energy,
     out_r, out_l, out_c,
     panel, kb, kf, xs, xb, img, wbuf, lhs_r, lhs_l, terms,
-    a0_send, a0_recv, a1_send, a1_recv, b_row, b_own, b_left, c_rsend, c_rrecv, c_lsend, c_lrecv, d_row,
+    a0_send, a0_recv, a1_send, a1_recv, b_row, b_own, b_left, c_rsend, c_rrecv, c_lsend, c_lrecv, d_r, d_l,
     e_send, e_recv, y_all, g_all, t_all,
     k_sem, p_up, p_dn, p_x, p_recv,
-    a_ss, a_rs, b_ss, b_rs, bl_ss, bl_rs, cr_ss, cr_rs, cl_ss, cl_rs, d_ss, d_rs,
+    a_ss, a_rs, b_ss, b_rs, bl_ss, bl_rs, cr_ss, cr_rs, cl_ss, cl_rs, dr_ss, dr_rs, dl_ss, dl_rs,
     e_ss, e_rs, y_ss, y_rs, g_ss, g_rs, t_ss, t_rs,
 ):
     row = lax.axis_index("row")
@@ -415,6 +415,20 @@
             def _():
                 remote(c_rsend.at[it, s], c_rrecv.at[it, col], cr_ss.at[it, s], cr_rs.at[it, col], own_row, own_col).start()
 
+        @pl.loop(1, R)
+        def _(k):
+            peer = away(k)
+            remote(c_lsend.at[it, peer], c_lrecv.at[it, peer], cl_ss.at[it, peer], cl_rs.at[it, peer], peer, col).wait_recv()
+        zl = c_lrecv[it, 0]
+        for j in range(1, R):
+            zl = zl + c_lrecv[it, j]
+        d_l[it, row] = zl
+
+        @pl.loop(1, R)
+        def _(k):
+            peer = away(k)
+            remote(d_l.at[it, row], d_l.at[it, row], dl_ss.at[it, peer], dl_rs.at[it, row], peer, col).start()
+
         for j in range(C):
             here = jnp.logical_and(owner_row == row, col == j)
 
@@ -422,27 +436,20 @@
             def _():
                 remote(c_rsend.at[it, j], c_rrecv.at[it, j], cr_ss.at[it, j], cr_rs.at[it, j], owner_row, j).wait_recv()
 
-        @pl.loop(1, R)
-        def _(k):
-            peer = away(k)
-            remote(c_lsend.at[it, peer], c_lrecv.at[it, peer], cl_ss.at[it, peer], cl_rs.at[it, peer], peer, col).wait_recv()
         zr = c_rrecv[it, 0]
         for j in range(1, C):
             zr = zr + c_rrecv[it, j]
-        zl = c_lrecv[it, 0]
-        for j in range(1, R):
-            zl = zl + c_lrecv[it, j]
-        d_row[it, row] = jnp.concatenate([zr, zl], axis=0)
-
-        @pl.loop(1, R)
-        def _(k):
-            peer = away(k)
-            remote(d_row.at[it, row], d_row.at[it, row], d_ss.at[it, peer], d_rs.at[it, row], peer, col).start()
-
-        @pl.loop(1, R)
-        def _(k):
-            peer = away(k)
-            remote(d_row.at[it, row], d_row.at[it, peer], d_ss.at[it, peer], d_rs.at[it, peer], peer, col).wait_recv()
+        d_r[it, row] = zr
+
+        @pl.loop(1, R)
+        def _(k):
+            peer = away(k)
+            remote(d_r.at[it, row], d_r.at[it, row], dr_ss.at[it, peer], dr_rs.at[it, row], peer, col).start()
+
+        @pl.loop(1, R)
+        def _(k):
+            peer = away(k)
+            remote(d_l.at[it, row], d_l.at[it, peer], dl_ss.at[it, peer], dl_rs.at[it, peer], peer, col).wait_recv()
 
         def e_copy(b):
             return remote(e_send.at[it, b], e_recv.at[it, b], e_ss.at[it, b], e_rs.at[it, b], row, mate)
@@ -460,10 +467,10 @@
         own = pl.ds(pl.multiple_of(core * half, half), half)
         rest = pl.ds(pl.multiple_of((1 - core) * half, half), half)
 
-        def backward(b):
+        def backward(b, zed, i):
             for j in range(R):
                 at = slice(j * chunk, (j + 1) * chunk)
-                z = d_row[it, j, pl.ds(b, 1), :]
+                z = zed[it, j, pl.ds(i, 1), :]
                 wbuf[:, at] = (cond[:, at].astype(f32) * z).astype(bf16)
             total = jnp.zeros((nc, nv), f32)
             for j in range(R):
@@ -491,19 +498,30 @@
             g_all[it, core, b] = total
             g_copy(b, core).start()
 
-        @pl.loop(0, stack)
-        def _(b):
-            backward(b)
-
-            @pl.when(b >= 1)
-            def _():
-                cross(b - 1)
-
-        cross(stack - 1)
-
-        @pl.loop(0, stack)
-        def _(b):
-            finish(b)
+        @pl.loop(0, count)
+        def _(k):
+            backward(count + k, d_l, k)
+
+            @pl.when(k >= 1)
+            def _():
+                cross(count + k - 1)
+
+        @pl.loop(1, R)
+        def _(k):
+            peer = away(k)
+            remote(d_r.at[it, row], d_r.at[it, peer], dr_ss.at[it, peer], dr_rs.at[it, peer], peer, col).wait_recv()
+
+        @pl.loop(0, count)
+        def _(k):
+            backward(k, d_r, k)
+            cross(lax.rem(k + stack - 1, stack))
+            finish(count + k)
+
+        cross(count - 1)
+
+        @pl.loop(0, count)
+        def _(k):
+            finish(k)
 
         @pl.loop(0, stack)
         def _(b):
@@ -587,7 +605,8 @@
             remote(a_send.at[peer], a_recv.at[row], a_ss.at[it, peer], a_rs.at[it, row], peer, col).wait_send()
             remote(b_row.at[it, row], b_row.at[it, row], b_ss.at[it, peer], b_rs.at[it, row], peer, col).wait_send()
             remote(c_lsend.at[it, peer], c_lrecv.at[it, row], cl_ss.at[it, peer], cl_rs.at[it, row], peer, col).wait_send()
-            remote(d_row.at[it, row], d_row.at[it, row], d_ss.at[it, peer], d_rs.at[it, row], peer, col).wait_send()
+            remote(d_r.at[it, row], d_r.at[it, row], dr_ss.at[it, peer], dr_rs.at[it, row], peer, col).wait_send()
+            remote(d_l.at[it, row], d_l.at[it, row], dl_ss.at[it, peer], dl_rs.at[it, row], peer, col).wait_send()
             remote(t_all.at[it + 1, row], t_all.at[it + 1, row], t_ss.at[it + 1, peer], t_rs.at[it + 1, row], peer, col).wait_send()
 
         for j in range(C):
@@ -667,7 +686,8 @@
         V((ITERS, C, count, chunk), f32),
         V((ITERS, R, count, chunk), f32),
         V((ITERS, R, count, chunk), f32),
-        V((ITERS, R, stack, chunk), f32),
+        V((ITERS, R, count, chunk), f32),
+        V((ITERS, R, count, chunk), f32),
         V((ITERS, stack, half, nv), f32),
         V((ITERS, stack, half, nv), f32),
         V((ITERS, Y, stack, half, nv), bf16),
@@ -679,6 +699,7 @@
         D((ITERS, R)), D((ITERS, R)),
         D((ITERS, C)), D((ITERS, C)),
         D((ITERS, C)), D((ITERS, C)),
+        D((ITERS, R)), D((ITERS, R)),
         D((ITERS, R)), D((ITERS, R)),
         D((ITERS, R)), D((ITERS, R)),
         D((ITERS, stack)), D((ITERS, stack)),

time: 133 us -> 128 us (0.962)
  Pallas kernels: 127 us -> 122 us
    pallas_call x1, Pallas kernels: 127 us -> 122 us  [fused(): pl.pallas_call(functools.partial(body_kernel, R, C), out_shape=(jax.Shape...]
where the time goes in v3:
time: 128 us; the launch traced here: 127 us
  Pallas kernels  122 us (95%)
  other arithmetic  3.76 us (3%)
  local copies, waits for them, and re-layouts  1.33 us (1%)
    pallas_call x1, Pallas kernels, fused(): pl.pallas_call(functools.partial(body_kernel, R, C), out_shape=(jax.Shape...  122 us

profile of v3, /device:TPU:0, one launch (start us, length us, event | category | flops | bytes accessed | tf_op | source)
XLA Modules:
  0.0 127.3 jit_solution(5261406578470437840)
XLA Ops:
  0.6 1.4 %broadcast_subtract_fusion.energy = f32[128,256]{1,0:T(8,128)} fusion(f32[256]{0:T(256)} %param.11, f32[128]{0:T(128)} %param.10), kind=kLoop, calls=%fused_computation.2 | loop fusion | flops 32768 | bytes 132608 | tf_op jit(solution)/shard_map/sub | solution.py:665
  2.1 121.6 %shard_map.85 = (f32[4,128,256]{2,1,0:T(8,128)}, f32[4,128,256]{2,1,0:T(8,128)}, f32[4,128]{1,0:T(4,128)}) custom-call(f32[4,128,256]{2,1,0:T(8,128)} %start.1, bf16[128,4096]{1,0:T(8,128)(2,1)} %cond.1, bf16[32,4096]{1,0:T(8,128)(2,1)} %val.1, f32[2048,4096]{1,0:T(8,128)} %kmat.1, f32[128,256]{1,0:T(8,128)} %broadcast_subtract_fusion.energy), custom_call_target="tpu_custom_call" | custom-call | tf_op jit(solution)/shard_map/pallas_call | solution.py:710
  123.6 0.7 slice_bitcast_fusion
  124.3 2.3 %broadcast_divide_fusion = (f32[4,128,256]{2,1,0:T(8,128)}, f32[4,128,256]{2,1,0:T(8,128)}) fusion(f32[4,128,256]{2,1,0:T(8,128)} %get-tuple-element.8, f32[4]{0:T(128)S(1)} %slice_bitcast_fusion.1, f32[4,128,256]{2,1,0:T(8,128)} %get-tuple-element.6), kind=kLoop, calls=%fused_computation | loop fusion | flops 262144 | bytes 2097168 | tf_op jit(solution)/shard_map/div | solution.py:726
  126.6 0.7 copy.9
  (1 shorter events, 0.0 us)

commit v4 on v3

--- a/solution.py
+++ b/solution.py
@@ -472,13 +472,10 @@
                 at = slice(j * chunk, (j + 1) * chunk)
                 z = zed[it, j, pl.ds(i, 1), :]
                 wbuf[:, at] = (cond[:, at].astype(f32) * z).astype(bf16)
-            total = jnp.zeros((nc, nv), f32)
-            for j in range(R):
-                at = slice(j * chunk, (j + 1) * chunk)
-                total = total + lax.dot_general(
-                    wbuf[:, at], panel[:, :, at].reshape(nv, chunk), (((1,), (1,)), ((), ())),
-                    preferred_element_type=f32,
-                )
+            total = lax.dot_general(
+                wbuf[...], panel[...].reshape(nv, R * chunk), (((1,), (1,)), ((), ())),
+                preferred_element_type=f32,
+            )
             img[b] = total
             e_send[it, b] = img[b, rest, :]
             e_copy(b).start()

time: 128 us -> 128 us (level)
  no operation moved by 1% of the time
where the time goes in v4:
time: 128 us; the launch traced here: 127 us
  Pallas kernels  122 us (95%)
  other arithmetic  3.76 us (3%)
  local copies, waits for them, and re-layouts  1.33 us (1%)
    pallas_call x1, Pallas kernels, fused(): pl.pallas_call(functools.partial(body_kernel, R, C), out_shape=(jax.Shape...  122 us

profile of v4, /device:TPU:0, one launch (start us, length us, event | category | flops | bytes accessed | tf_op | source)
XLA Modules:
  0.0 127.4 jit_solution(14732457384297122643)
XLA Ops:
  0.6 1.4 %broadcast_subtract_fusion.energy = f32[128,256]{1,0:T(8,128)} fusion(f32[256]{0:T(256)} %param.11, f32[128]{0:T(128)} %param.10), kind=kLoop, calls=%fused_computation.2 | loop fusion | flops 32768 | bytes 132608 | tf_op jit(solution)/shard_map/sub | solution.py:662
  2.1 121.7 %shard_map.85 = (f32[4,128,256]{2,1,0:T(8,128)}, f32[4,128,256]{2,1,0:T(8,128)}, f32[4,128]{1,0:T(4,128)}) custom-call(f32[4,128,256]{2,1,0:T(8,128)} %start.1, bf16[128,4096]{1,0:T(8,128)(2,1)} %cond.1, bf16[32,4096]{1,0:T(8,128)(2,1)} %val.1, f32[2048,4096]{1,0:T(8,128)} %kmat.1, f32[128,256]{1,0:T(8,128)} %broadcast_subtract_fusion.energy), custom_call_target="tpu_custom_call" | custom-call | tf_op jit(solution)/shard_map/pallas_call | solution.py:707
  123.8 0.7 slice_bitcast_fusion
  124.4 2.3 %broadcast_divide_fusion = (f32[4,128,256]{2,1,0:T(8,128)}, f32[4,128,256]{2,1,0:T(8,128)}) fusion(f32[4,128,256]{2,1,0:T(8,128)} %get-tuple-element.8, f32[4]{0:T(128)S(1)} %slice_bitcast_fusion.1, f32[4,128,256]{2,1,0:T(8,128)} %get-tuple-element.6), kind=kLoop, calls=%fused_computation | loop fusion | flops 262144 | bytes 2097168 | tf_op jit(solution)/shard_map/div | solution.py:723
  126.8 0.7 copy.9
  (1 shorter events, 0.0 us)
